TPU v7x, 32 devices: a whole 2x2x4 slice. The times are simulated.
32 devices in a mesh: groups: 2 (over y), seq: 4 (over z), head: 2 (over x), batch: 2 (over core).
Axes of the slice: x: 2, y: 2, z: 4, core: 2. Of those that a mesh axis runs over, the one named last changes fastest.
Arguments:
- queries: bfloat16 [4, 512, 2560], P(('groups', 'batch'), 'seq', 'head'), parts along dimension 0, may hold values from -6 to 6
- keys: bfloat16 [4, 512, 2560], P(('groups', 'batch'), 'seq', 'head'), parts along dimension 0, may hold values from -6 to 6
- values: bfloat16 [4, 512, 2560], P(('groups', 'batch'), 'seq', 'head'), parts along dimension 0, may hold values from -6 to 6
- cache_keys: bfloat16 [4, 8, 32, 2560], P(('groups', 'batch'), 'seq', None, 'head'), parts along dimension 0, may hold values from -6 to 6
- cache_values: bfloat16 [4, 8, 32, 2560], P(('groups', 'batch'), 'seq', None, 'head'), parts along dimension 0, may hold values from -6 to 6
- frame_list: int32 [4, 3], P(('groups', 'batch')), parts along dimension 0, may hold values from 0 to 7, as said below
- frame_place: int32 [4, 8], P(('groups', 'batch')), parts along dimension 0, may hold values from 0 to 7, each once within a row
- tile_mask: int32 [4, 4, 4], P(('groups', 'batch'), 'seq'), parts along dimension 0, may hold values from 0 to 1, as said below
Outputs:
- attention: bfloat16 [4, 512, 2560], P(('groups', 'batch'), 'seq', 'head'), parts along dimension 0
There are 2 independent parts, one for each index of `groups`. A program takes and returns all parts, laid end to end along the dimension named above; each array names one. Nothing has to cross between parts.
Inputs may be any that keep to these rules, and one draw needn't show every extreme that they name: `frame_list`: each row holds frame 0 and then 3 - 1 consecutive frame numbers. `tile_mask`: ones on the diagonal of each video's tile matrix.
All inputs are finite; a program needn't handle non-finite values.
Results may differ from a plain program's by a relative error of at most 0.006.
Values may be sent and summed in bfloat16 or wider, within the bound.
No kernel may reach another device: no remote copies, remote signals or barrier semaphores. Data moves between devices by JAX's collectives and lax.ppermute only.
A program may use at most 128 MiB of HBM per device.

v0:
```python
import math
import jax
import jax.numpy as jnp
from jax import lax
from jax.sharding import PartitionSpec as P

HD = 128
TILE = 128
NEG_FILL = -1e30


def attend(running, key_part, value_part, live, query_heads):
    videos, length, col_count = key_part.shape
    head_count = col_count // HD

    def update(previous):
        peak_old, total_old, summed_old = previous
        key_heads = key_part.reshape(videos, length, head_count, HD)
        value_heads = value_part.reshape(videos, length, head_count, HD)
        scores = jnp.einsum(
            "vqhd,vkhd->vhqk", query_heads, key_heads, preferred_element_type=jnp.float32
        ) * (1.0 / math.sqrt(HD))
        allowed = live[:, None, :, :]
        scores = jnp.where(allowed, scores, NEG_FILL)
        peak_new = jnp.maximum(peak_old, jnp.max(scores, axis=3))
        weights = jnp.where(allowed, jnp.exp(scores - peak_new[..., None]), 0.0)
        factor = jnp.exp(peak_old - peak_new)
        total_new = total_old * factor + jnp.sum(weights, axis=3)
        product = jnp.einsum(
            "vhqk,vkhd->vhqd",
            weights.astype(jnp.bfloat16),
            value_heads,
            preferred_element_type=jnp.float32,
        )
        summed_new = summed_old * factor[..., None] + product
        return (peak_new, total_new, summed_new)

    def unchanged(previous):
        return previous

    return lax.cond(jnp.any(live), update, unchanged, running)


def body(queries, keys, values, cache_keys, cache_values, frame_list, frame_place, tile_mask):
    videos, tok_rows, col_count = queries.shape
    head_count = col_count // HD
    query_heads = queries.reshape(videos, tok_rows, head_count, HD)
    running = (
        jnp.full((videos, head_count, tok_rows), NEG_FILL, jnp.float32),
        jnp.zeros((videos, head_count, tok_rows), jnp.float32),
        jnp.zeros((videos, head_count, tok_rows, HD), jnp.float32),
    )
    frame_tok = cache_keys.shape[2]
    listed = jnp.any(frame_place[:, :, None] == frame_list[:, None, :], axis=2)
    key_piece = lax.all_gather(cache_keys, "seq", axis=1, tiled=True)
    value_piece = lax.all_gather(cache_values, "seq", axis=1, tiled=True)
    count_frames = key_piece.shape[1]
    token_flags = jnp.repeat(listed, frame_tok, axis=1)
    live = jnp.broadcast_to(token_flags[:, None, :], (videos, tok_rows, count_frames * frame_tok))
    key_flat = key_piece.reshape(videos, count_frames * frame_tok, col_count)
    value_flat = value_piece.reshape(videos, count_frames * frame_tok, col_count)
    running = attend(running, key_flat, value_flat, live, query_heads)
    key_piece = lax.all_gather(keys, "seq", axis=1, tiled=True)
    value_piece = lax.all_gather(values, "seq", axis=1, tiled=True)
    length = key_piece.shape[1]
    key_tiles = jnp.arange(length, dtype=jnp.int32) // TILE
    tile_live = jnp.take(tile_mask, key_tiles, axis=2)
    running = attend(
        running, key_piece, value_piece, jnp.repeat(tile_live, TILE, axis=1) > 0, query_heads
    )
    peak, total, summed = running
    result = summed / total[..., None]
    return result.transpose(0, 2, 1, 3).reshape(videos, tok_rows, col_count).astype(jnp.bfloat16)


def solution(mesh):
    return jax.shard_map(
        body,
        mesh=mesh,
        in_specs=(
            P(("groups", "batch"), "seq", "head"),
            P(("groups", "batch"), "seq", "head"),
            P(("groups", "batch"), "seq", "head"),
            P(("groups", "batch"), "seq", None, "head"),
            P(("groups", "batch"), "seq", None, "head"),
            P(("groups", "batch"), None),
            P(("groups", "batch"), None),
            P(("groups", "batch"), "seq", None),
        ),
        out_specs=P(("groups", "batch"), "seq", "head"),
        check_vma=False,
    )
```

profile of v0, /device:TPU:0, one launch (start us, length us, event | category | flops | bytes accessed | tf_op | source)
XLA Modules:
  0.0 110.2 jit_solution(18014833076720647111)
XLA Ops:
  6.5 0.0 copy-start.3
  6.5 0.0 copy-start.5
  6.5 0.0 copy-start.6
  6.5 0.0 copy-start
  6.5 0.0 copy-start.1
  6.5 0.0 all-gather.3.cloned.1.call-start
  6.6 1.9 %copy.50 = bf16[1,128,1280]{1,2,0:T(8,128)(2,1)} copy(bf16[1,128,1280]{2,1,0:T(8,128)(2,1)} %param.13) | data formatting | bytes 655360 | tf_op args[1]
  8.5 0.0 all-gather.3.cloned.1.call-update
  8.6 0.0 copy-start.2
  8.6 0.0 all-gather.5.cloned.1.call-start
  8.6 1.9 %copy.51 = bf16[1,128,1280]{1,2,0:T(8,128)(2,1)} copy(bf16[1,128,1280]{2,1,0:T(8,128)(2,1)} %param.14) | data formatting | bytes 655360 | tf_op args[2]
  10.5 0.0 all-gather.5.cloned.1.call-update
  10.5 0.0 copy-done.3
  10.6 0.7 fusion.41
  11.2 2.7 %compare_select_fusion.1 = s32[512,1]{0,1:T(1,128)S(1)} fusion(s32[]{:T(128)} %bitcast.15, s32[]{:T(128)} %bitcast.16, s32[]{:T(128)} %bitcast.18, s32[]{:T(128)} %bitcast.17), kind=kLoop, calls=%fused_computation.45 | loop fusion | flops 8704 | bytes 2064 | tf_op jit(solution)/shard_map/jit(_take)/gather | solution.py:67
  14.0 0.8 broadcast_reduce_fusion
  15.4 0.0 copy-done.5
  15.4 0.0 copy-done.6
  15.4 0.1 compare_reduce_fusion
  15.5 0.1 broadcast_in_dim.88
  15.6 0.1 broadcast_in_dim.89
  15.7 0.7 broadcast_reduce_fusion.1
  17.1 0.0 copy-done
  17.2 0.2 copy.44
  17.4 0.0 copy-done.1
  17.4 27.2 %all_gather.12 = bf16[1,8,32,1280]{3,2,0,1:T(8,128)(2,1)S(1)} all-gather(bf16[1,2,32,1280]{3,2,0,1:T(8,128)(2,1)S(1)} %bitcast.73), channel_id=1, replica_groups=mesh['groups'=2,'seq'=4,'head'=2,'batch'=2] {'seq'}, dimensions={1}, use_global_device_ids=true | all-gather | bytes 819200 | tf_op jit(solution)/shard_map/all_gather | solution.py:55
  44.6 0.0 copy-done.2
  44.6 21.8 %all_gather.13 = bf16[1,8,32,1280]{3,2,0,1:T(8,128)(2,1)S(1)} all-gather(bf16[1,2,32,1280]{3,2,0,1:T(8,128)(2,1)S(1)} %bitcast.74), channel_id=1, replica_groups=mesh['groups'=2,'seq'=4,'head'=2,'batch'=2] {'seq'}, dimensions={1}, use_global_device_ids=true | all-gather | bytes 819200 | tf_op jit(solution)/shard_map/all_gather | solution.py:56
  66.3 3.3 %conditional.2 = (f32[1,10,128]{2,1,0:T(8,128)S(1)}, f32[1,10,128]{2,1,0:T(8,128)S(1)}, f32[1,10,128,128]{3,2,1,0:T(8,128)}) conditional(s32[]{:T(128)} %convert_element_type.32, () %tuple.20, (pred[8]{0:T(512)(128)(4,1)S(1)}, bf16[1,128,10,128]{1,3,2,0:T(8,128)(2,1)S(1)}, bf16[1,8,32,1280]{3,2,0,1:T(8,128)(2,1)S(1)}, ...), branch_computations={%region_3.4_spmd, %region_4.7_spmd} | conditional | flops 170891520 | bytes 8910368 | solution.py:41
  66.3 0.4 reshape.260
  66.7 0.1 broadcast_in_dim.71
  66.8 0.1 reshape.258
  66.9 0.5 fusion.40
  67.4 0.5 fusion.3
  67.9 0.4 reshape.261
  68.3 1.3 %fusion.1 = f32[1,10,128,128]{3,2,1,0:T(8,128)} fusion(f32[10,128,256]{2,1,0:T(8,128)S(1)} %get-tuple-element.99, bf16[256,10,128]{2,1,0:T(8,128)(2,1)S(1)} %reshape.261, f32[10,128]{1,0:T(8,128)S(1)} %get-tuple-element.97, pred[256]{0:T(512)(128)(4,1)S(1)} %reshape.258, f32[10,128]{1,0:T(8,128)S(1)} %get-tuple-element.96), kind=kOutput, calls=%fused_computation.4 | convolution fusion | flops 85032960 | bytes 2631936 | tf_op jit(solution)/shard_map/cond/branch_1_fun/vhqk,vkhd->vhqd/dot_general | solution.py:29
  69.6 0.0 all-gather.3.cloned.1.call-done
  69.6 26.9 %all-gather.5.cloned.1.call-done = bf16[1,512,1280]{1,2,0:T(8,128)(2,1)} async-done(((bf16[1,128,1280]{1,2,0:T(8,128)(2,1)}), bf16[1,512,1280]{1,2,0:T(8,128)(2,1)}) %all-gather.5.cloned.1.call-update) | async-done | bytes 1310736 | tf_op jit(solution)/shard_map/all_gather | solution.py:64
  96.6 5.8 %conditional.3 = (f32[1,10,128]{2,1,0:T(8,128)S(1)}, f32[1,10,128,128]{2,3,1,0:T(8,128)S(1)}) conditional(s32[]{:T(128)} %convert_element_type.31, (f32[1,10,128]{2,1,0:T(8,128)S(1)}, f32[1,10,128,128]{3,2,1,0:T(8,128)}) %tuple.22, (pred[1,128,512]{2,1,0:T(8,128)(4,1)S(1)}, bf16[1,128,10,128]{1,3,2,0:T(8,128)(2,1)S(1)}, ...), branch_computations={%region_7.8_spmd, %region_8.11_spmd} | conditional | flops 344396800 | bytes 18946092 | solution.py:41
  96.6 2.0 %fusion.13 = (f32[10,128]{1,0:T(8,128)S(1)}, f32[10,128,512]{2,1,0:T(8,128)S(1)}) fusion(pred[128,512]{1,0:T(8,128)(4,1)S(1)} %bitcast.70, bf16[512,10,128]{0,2,1:T(8,128)(2,1)} %bitcast.68, bf16[1,128,10,128]{1,3,2,0:T(8,128)(2,1)S(1)} %get-tuple-element.81), kind=kOutput, calls=%fused_computation.20 | convolution fusion | flops 169736960 | bytes 4330496 | tf_op jit(solution)/shard_map/cond/branch_1_fun/vqhd,vkhd->vhqk/dot_general | solution.py:20
  98.6 0.0 copy-start.4
  98.7 0.9 fusion.15
  99.5 0.4 copy-done.4
  100.0 2.2 %fusion.26 = f32[1,10,128,128]{3,2,1,0:T(8,128)S(1)} fusion(bf16[512,10,128]{0,2,1:T(8,128)(2,1)S(1)} %bitcast.77, f32[10,128,512]{2,1,0:T(8,128)S(1)} %get-tuple-element.95, f32[10,128]{1,0:T(8,128)S(1)} %get-tuple-element.93, pred[128,512]{1,0:T(8,128)(4,1)S(1)} %bitcast.72, f32[1,10,128,128]{3,2,1,0:T(8,128)} %get-tuple-element.42, ...), kind=kOutput, calls=%fused_computation.30 | convolution fusion | flops 171376640 | bytes 5318656 | tf_op jit(solution)/shard_map/cond/branch_1_fun/vhqk,vkhd->vhqd/dot_general | solution.py:29
  102.1 0.2 copy.58
  102.4 0.1 divide_convert_fusion
  102.4 0.9 copy.54
  (6 shorter events, 0.1 us)
Async XLA Ops:
  6.5 4.0 %copy-start.3 = (s32[1,1,4]{2,1,0:T(1,128)S(1)}, s32[1,1,4]{2,1,0:T(1,128)}, u32[]{:S(2)}) copy-start(s32[1,1,4]{2,1,0:T(1,128)} %param.19) | copy-start | bytes 52
  6.5 8.9 %copy-start.5 = (s32[1,8]{1,0:T(1,128)S(1)}, s32[1,8]{1,0:T(1,128)}, u32[]{:S(2)}) copy-start(s32[1,8]{1,0:T(1,128)} %param.18) | copy-start | bytes 100
  6.5 8.9 %copy-start.6 = (s32[1,3]{1,0:T(1,128)S(1)}, s32[1,3]{1,0:T(1,128)}, u32[]{:S(2)}) copy-start(s32[1,3]{1,0:T(1,128)} %param.17) | copy-start | bytes 40
  6.5 10.6 %copy-start = (bf16[1,128,1280]{2,1,0:T(8,128)(2,1)S(1)}, bf16[1,128,1280]{2,1,0:T(8,128)(2,1)}, u32[]{:S(2)}) copy-start(bf16[1,128,1280]{2,1,0:T(8,128)(2,1)} %param.12) | copy-start | bytes 983044
  6.5 10.8 %copy-start.1 = (bf16[1,2,32,1280]{3,2,1,0:T(8,128)(2,1)S(1)}, bf16[1,2,32,1280]{3,2,1,0:T(8,128)(2,1)}, u32[]{:S(2)}) copy-start(bf16[1,2,32,1280]{3,2,1,0:T(8,128)(2,1)} %param.15) | copy-start | bytes 491524
  6.5 63.1 %all-gather.3.cloned.1.call-start = ((), (), s32[]{:S(2)}) async-start(), calls=%async_computation | async-start | bytes 1638400 | tf_op jit(solution)/shard_map/all_gather | solution.py:63
  8.6 36.0 %copy-start.2 = (bf16[1,2,32,1280]{3,2,1,0:T(8,128)(2,1)S(1)}, bf16[1,2,32,1280]{3,2,1,0:T(8,128)(2,1)}, u32[]{:S(2)}) copy-start(bf16[1,2,32,1280]{3,2,1,0:T(8,128)(2,1)} %param.16) | copy-start | bytes 491524
  8.6 88.0 %all-gather.5.cloned.1.call-start = ((), (), s32[]{:S(2)}) async-start(), calls=%async_computation.1 | async-start | bytes 1638400 | tf_op jit(solution)/shard_map/all_gather | solution.py:64
  98.6 1.3 %copy-start.4 = (bf16[1,512,1280]{1,2,0:T(8,128)(2,1)S(1)}, bf16[1,512,1280]{1,2,0:T(8,128)(2,1)}, u32[]{:S(2)}) copy-start(bf16[1,512,1280]{1,2,0:T(8,128)(2,1)} %get-tuple-element.43) | copy-start | bytes 3932164 | tf_op jit(solution)/shard_map/cond
Sparse Core Ops, SparseCore 0:
  8.9 54.7 all-gather.2
  65.3 31.2 all-gather.4
where the time goes:
time: 111 us; the launch traced here: 110 us
  blocking collectives  49 us (44%)
  waiting for transfers between devices  27 us (24%)
  between operations  14.9 us (13%)
  local copies, waits for them, and re-layouts  7.46 us (7%)
  matrix products  5.99 us (5%)
  other arithmetic  5.75 us (5%)
    all_gather x1, blocking collectives, body(): key_piece = lax.all_gather(cache_keys, 'seq', axis=1, tiled=True)  27.2 us
    all_gather x1, waiting for transfers between devices, body(): value_piece = lax.all_gather(values, 'seq', axis=1, tiled=True)  26.9 us
    all_gather x1, blocking collectives, body(): value_piece = lax.all_gather(cache_values, 'seq', axis=1, tiled=True)  21.8 us
    unnamed x15, local copies, waits for them, and re-layouts  4.08 us
    dot_general x2, matrix products, update(): jnp.einsum('vhqk,vkhd->vhqd', weights.astype(jnp.bfloat16), value_heads,...  3.49 us
    gather x1, other arithmetic, body(): tile_live = jnp.take(tile_mask, key_tiles, axis=2)  2.7 us
    dot_general x2, matrix products, update(): jnp.einsum('vqhd,vkhd->vhqk', query_heads, key_heads, preferred_element_t...  2.5 us
  transfers between devices with their start and end apart: 2, of which 1 were waited for; matrix products, arithmetic and copies ran while one was open for 10% of the time, Pallas kernels for 0%

commit v1 on v0

--- a/solution.py
+++ b/solution.py
@@ -52,8 +52,13 @@
     )
     frame_tok = cache_keys.shape[2]
     listed = jnp.any(frame_place[:, :, None] == frame_list[:, None, :], axis=2)
-    key_piece = lax.all_gather(cache_keys, "seq", axis=1, tiled=True)
-    value_piece = lax.all_gather(cache_values, "seq", axis=1, tiled=True)
+    key_piece, value_piece = jnp.split(
+        lax.all_gather(
+            jnp.concatenate([cache_keys, cache_values], axis=0), "seq", axis=1, tiled=True
+        ),
+        [cache_keys.shape[0]],
+        axis=0,
+    )
     count_frames = key_piece.shape[1]
     token_flags = jnp.repeat(listed, frame_tok, axis=1)
     live = jnp.broadcast_to(token_flags[:, None, :], (videos, tok_rows, count_frames * frame_tok))

time: 111 us -> 126 us (1.14)
  waiting for transfers between devices: 27 us -> 89.7 us
  blocking collectives: 49 us -> 0 us
  other arithmetic: 5.75 us -> 7.22 us
    all_gather x2 -> x0, blocking collectives: 49 us -> none  [the longest x1 27.2 us: body(): key_piece = lax.all_gather(cache_keys, 'seq', axis=1, tiled=True)]
    all_gather x1, waiting for transfers between devices: 0.01 us -> 29.4 us  [body(): key_piece = lax.all_gather(keys, 'seq', axis=1, tiled=True)]
    all_gather x0 -> x1, waiting for transfers between devices: none -> 26.7 us  [body(): lax.all_gather(jnp.concatenate([cache_keys, cache_values], axis=0), 'seq'...]
    all_gather x1, waiting for transfers between devices: 26.9 us -> 33.6 us  [body(): value_piece = lax.all_gather(values, 'seq', axis=1, tiled=True)]
    concatenate x0 -> x1, other arithmetic: none -> 1.8 us  [body(): jnp.concatenate([cache_keys, cache_values], axis=0)]
    split x0 -> x1, local copies, waits for them, and re-layouts: none -> 1.37 us  [body(): jnp.split(lax.all_gather(jnp.concatenate([cache_keys, cache_values], axis...]
    unnamed x15 -> x13, local copies, waits for them, and re-layouts: 4.08 us -> 3.05 us
  transfers between devices with their start and end apart: 2 -> 3, of which waited for: 1 -> 3; matrix products, arithmetic and copies ran while one was open for 10% -> 10% of each run, Pallas kernels for 0% -> 0%
where the time goes in v1:
time: 126 us; the launch traced here: 125 us
  waiting for transfers between devices  89.7 us (71%)
  between operations  14.4 us (11%)
  local copies, waits for them, and re-layouts  7.78 us (6%)
  other arithmetic  7.22 us (6%)
  matrix products  5.98 us (5%)
    all_gather x1, waiting for transfers between devices, body(): value_piece = lax.all_gather(values, 'seq', axis=1, tiled=True)  33.6 us
    all_gather x1, waiting for transfers between devices, body(): key_piece = lax.all_gather(keys, 'seq', axis=1, tiled=True)  29.4 us
    all_gather x1, waiting for transfers between devices, body(): lax.all_gather(jnp.concatenate([cache_keys, cache_values], axis=0), 'seq'...  26.7 us
    dot_general x2, matrix products, update(): jnp.einsum('vhqk,vkhd->vhqd', weights.astype(jnp.bfloat16), value_heads,...  3.48 us
    unnamed x13, local copies, waits for them, and re-layouts  3.05 us
  transfers between devices with their start and end apart: 3, of which 3 were waited for; matrix products, arithmetic and copies ran while one was open for 10% of the time, Pallas kernels for 0%

profile of v1, /device:TPU:0, one launch (start us, length us, event | category | flops | bytes accessed | tf_op | source)
XLA Modules:
  0.0 125.3 jit_solution(14365211495413838437)
XLA Ops:
  6.5 0.0 copy-start
  6.5 0.0 all-gather.4.cloned.1.call-start
  6.5 1.8 %pad_maximum_fusion = bf16[2,2,32,1280]{3,2,1,0:T(8,128)(2,1)} fusion(bf16[1,2,32,1280]{3,2,1,0:T(8,128)(2,1)} %param.16, bf16[1,2,32,1280]{3,2,1,0:T(8,128)(2,1)} %param.15), kind=kLoop, calls=%fused_computation.42 | loop fusion | flops 163840 | bytes 655360 | tf_op jit(solution)/shard_map/concatenate | solution.py:57
  8.3 0.0 copy-start.2
  8.3 0.0 copy-start.4
  8.3 0.0 copy-start.5
  8.3 0.0 copy-start.1
  8.3 0.0 all-gather.4.cloned.1.call-update
  8.4 0.0 all-gather.6.cloned.1.call-start
  8.4 1.9 %copy.29 = bf16[1,128,1280]{1,2,0:T(8,128)(2,1)} copy(bf16[1,128,1280]{2,1,0:T(8,128)(2,1)} %param.13) | data formatting | bytes 655360 | tf_op args[1]
  10.3 0.0 all-gather.6.cloned.1.call-update
  10.4 0.0 all-gather.8.cloned.1.call-start
  10.4 0.0 copy-done
  10.4 0.9 copy.30
  11.3 0.0 all-gather.8.cloned.1.call-update
  11.4 0.0 copy-done.2
  11.4 0.6 fusion.42
  12.0 2.4 %compare_select_fusion.1 = s32[512,1]{0,1:T(1,128)S(1)} fusion(s32[]{:T(128)} %bitcast.13, s32[]{:T(128)} %bitcast.14, s32[]{:T(128)} %bitcast.16, s32[]{:T(128)} %bitcast.15), kind=kLoop, calls=%fused_computation.46 | loop fusion | flops 8704 | bytes 2064 | tf_op jit(solution)/shard_map/jit(_take)/gather | solution.py:72
  14.5 0.8 broadcast_reduce_fusion
  15.8 0.0 copy-done.4
  15.9 0.0 copy-done.5
  15.9 0.1 compare_reduce_fusion
  16.0 0.1 broadcast_in_dim.88
  16.0 0.1 broadcast_in_dim.89
  16.1 0.7 broadcast_reduce_fusion.1
  17.5 0.0 copy-done.1
  17.5 0.2 copy.27
  17.7 26.7 %all-gather.4.cloned.1.call-done = bf16[2,8,32,1280]{3,2,1,0:T(8,128)(2,1)} async-done(((bf16[2,2,32,1280]{3,2,1,0:T(8,128)(2,1)}), bf16[2,8,32,1280]{3,2,1,0:T(8,128)(2,1)}) %all-gather.4.cloned.1.call-update) | async-done | bytes 1310736 | tf_op jit(solution)/shard_map/all_gather | solution.py:56
  44.4 4.6 %conditional.2 = (f32[1,10,128]{2,1,0:T(8,128)S(1)}, f32[1,10,128]{2,1,0:T(8,128)S(1)}, f32[1,10,128,128]{3,2,1,0:T(8,128)}) conditional(s32[]{:T(128)} %convert_element_type.32, () %tuple.20, (pred[8]{0:T(512)(128)(4,1)S(1)}, bf16[1,128,10,128]{1,3,2,0:T(8,128)(2,1)S(1)}, bf16[2,8,32,1280]{3,2,1,0:T(8,128)(2,1)}) %tuple.49), branch_computations={%region_3.4_spmd, %region_4.7_spmd} | conditional | flops 170891520 | bytes 11531808 | solution.py:41
  44.4 1.4 %fusion.40 = (bf16[1,8,32,1280]{3,2,1,0:T(8,128)(2,1)S(1)}, bf16[1,8,32,1280]{3,2,1,0:T(8,128)(2,1)S(1)}) fusion(bf16[2,8,32,1280]{3,2,1,0:T(8,128)(2,1)} %get-tuple-element.36), kind=kLoop, calls=%fused_computation.63 | loop fusion | bytes 2621440 | tf_op jit(solution)/shard_map/split | solution.py:55
  45.7 0.4 reshape.260
  46.1 0.1 broadcast_in_dim.71
  46.2 0.1 reshape.258
  46.3 0.5 fusion.41
  46.8 0.5 fusion.3
  47.3 0.4 reshape.261
  47.7 1.3 %fusion.1 = f32[1,10,128,128]{3,2,1,0:T(8,128)} fusion(f32[10,128,256]{2,1,0:T(8,128)S(1)} %get-tuple-element.88, bf16[256,10,128]{2,1,0:T(8,128)(2,1)S(1)} %reshape.261, f32[10,128]{1,0:T(8,128)S(1)} %get-tuple-element.86, pred[256]{0:T(512)(128)(4,1)S(1)} %reshape.258, f32[10,128]{1,0:T(8,128)S(1)} %get-tuple-element.85), kind=kOutput, calls=%fused_computation.4 | convolution fusion | flops 85032960 | bytes 2631936 | tf_op jit(solution)/shard_map/cond/branch_1_fun/vhqk,vkhd->vhqd/dot_general | solution.py:29
  49.0 29.4 %all-gather.6.cloned.1.call-done = bf16[1,512,1280]{1,2,0:T(8,128)(2,1)} async-done(((bf16[1,128,1280]{1,2,0:T(8,128)(2,1)}), bf16[1,512,1280]{1,2,0:T(8,128)(2,1)}) %all-gather.6.cloned.1.call-update) | async-done | bytes 1310736 | tf_op jit(solution)/shard_map/all_gather | solution.py:68
  78.4 33.6 %all-gather.8.cloned.1.call-done = bf16[1,512,1280]{1,2,0:T(8,128)(2,1)} async-done(((bf16[1,128,1280]{1,2,0:T(8,128)(2,1)}), bf16[1,512,1280]{1,2,0:T(8,128)(2,1)}) %all-gather.8.cloned.1.call-update) | async-done | bytes 1310736 | tf_op jit(solution)/shard_map/all_gather | solution.py:69
  112.0 5.8 %conditional.3 = (f32[1,10,128]{2,1,0:T(8,128)S(1)}, f32[1,10,128,128]{2,3,1,0:T(8,128)S(1)}) conditional(s32[]{:T(128)} %convert_element_type.31, (f32[1,10,128]{2,1,0:T(8,128)S(1)}, f32[1,10,128,128]{3,2,1,0:T(8,128)}) %tuple.22, (pred[1,128,512]{2,1,0:T(8,128)(4,1)S(1)}, bf16[1,128,10,128]{1,3,2,0:T(8,128)(2,1)S(1)}, ...), branch_computations={%region_7.8_spmd, %region_8.11_spmd} | conditional | flops 344396800 | bytes 18946092 | solution.py:41
  112.0 2.0 %fusion.13 = (f32[10,128]{1,0:T(8,128)S(1)}, f32[10,128,512]{2,1,0:T(8,128)S(1)}) fusion(pred[128,512]{1,0:T(8,128)(4,1)S(1)} %bitcast.64, bf16[512,10,128]{0,2,1:T(8,128)(2,1)} %bitcast.62, bf16[1,128,10,128]{1,3,2,0:T(8,128)(2,1)S(1)} %get-tuple-element.68), kind=kOutput, calls=%fused_computation.20 | convolution fusion | flops 169736960 | bytes 4330496 | tf_op jit(solution)/shard_map/cond/branch_1_fun/vqhd,vkhd->vhqk/dot_general | solution.py:20
  114.1 0.0 copy-start.3
  114.1 0.9 fusion.15
  114.9 0.4 copy-done.3
  115.4 2.2 %fusion.26 = f32[1,10,128,128]{3,2,1,0:T(8,128)S(1)} fusion(bf16[512,10,128]{0,2,1:T(8,128)(2,1)S(1)} %bitcast.69, f32[10,128,512]{2,1,0:T(8,128)S(1)} %get-tuple-element.82, f32[10,128]{1,0:T(8,128)S(1)} %get-tuple-element.80, pred[128,512]{1,0:T(8,128)(4,1)S(1)} %bitcast.66, f32[1,10,128,128]{3,2,1,0:T(8,128)} %get-tuple-element.42, ...), kind=kOutput, calls=%fused_computation.30 | convolution fusion | flops 171376640 | bytes 5318656 | tf_op jit(solution)/shard_map/cond/branch_1_fun/vhqk,vkhd->vhqd/dot_general | solution.py:29
  117.5 0.2 copy.37
  117.8 0.1 divide_convert_fusion
  117.8 0.9 copy.33
  (6 shorter events, 0.1 us)
Async XLA Ops:
  6.5 3.9 %copy-start = (bf16[1,128,1280]{2,1,0:T(8,128)(2,1)S(1)}, bf16[1,128,1280]{2,1,0:T(8,128)(2,1)}, u32[]{:S(2)}) copy-start(bf16[1,128,1280]{2,1,0:T(8,128)(2,1)} %param.14) | copy-start | bytes 983044
  6.5 37.8 %all-gather.4.cloned.1.call-start = ((), (), s32[]{:S(2)}) async-start(), calls=%async_computation | async-start | bytes 1638400 | tf_op jit(solution)/shard_map/all_gather | solution.py:56
  8.3 3.0 %copy-start.2 = (s32[1,1,4]{2,1,0:T(1,128)S(1)}, s32[1,1,4]{2,1,0:T(1,128)}, u32[]{:S(2)}) copy-start(s32[1,1,4]{2,1,0:T(1,128)} %param.19) | copy-start | bytes 52
  8.3 7.5 %copy-start.4 = (s32[1,8]{1,0:T(1,128)S(1)}, s32[1,8]{1,0:T(1,128)}, u32[]{:S(2)}) copy-start(s32[1,8]{1,0:T(1,128)} %param.18) | copy-start | bytes 100
  8.3 7.5 %copy-start.5 = (s32[1,3]{1,0:T(1,128)S(1)}, s32[1,3]{1,0:T(1,128)}, u32[]{:S(2)}) copy-start(s32[1,3]{1,0:T(1,128)} %param.17) | copy-start | bytes 40
  8.3 9.1 %copy-start.1 = (bf16[1,128,1280]{2,1,0:T(8,128)(2,1)S(1)}, bf16[1,128,1280]{2,1,0:T(8,128)(2,1)}, u32[]{:S(2)}) copy-start(bf16[1,128,1280]{2,1,0:T(8,128)(2,1)} %param.12) | copy-start | bytes 983044
  8.4 70.0 %all-gather.6.cloned.1.call-start = ((), (), s32[]{:S(2)}) async-start(), calls=%async_computation.1 | async-start | bytes 1638400 | tf_op jit(solution)/shard_map/all_gather | solution.py:68
  10.4 101.6 %all-gather.8.cloned.1.call-start = ((), (), s32[]{:S(2)}) async-start(), calls=%async_computation.2 | async-start | bytes 1638400 | tf_op jit(solution)/shard_map/all_gather | solution.py:69
  114.1 1.3 %copy-start.3 = (bf16[1,512,1280]{1,2,0:T(8,128)(2,1)S(1)}, bf16[1,512,1280]{1,2,0:T(8,128)(2,1)}, u32[]{:S(2)}) copy-start(bf16[1,512,1280]{1,2,0:T(8,128)(2,1)} %get-tuple-element.43) | copy-start | bytes 3932164 | tf_op jit(solution)/shard_map/cond
Sparse Core Ops, SparseCore 0:
  8.9 35.3 all-gather.3
  45.9 32.4 all-gather.5
  80.0 31.9 all-gather.7
